TPU v7x, 32 devices: a whole 2x2x4 slice. The times are simulated.
32 devices in a mesh: groups: 2 (over x), grid: 16 (over z, y, core).
Axes of the slice: x: 2, y: 2, z: 4, core: 2. Of those that a mesh axis runs over, the one named last changes fastest.
Arguments:
- hist: float32 [768, 256, 256], P('groups', 'grid'), parts along dimension 0, may hold values from 0.2 to 2
- drift: float32 [2, 256, 256], P(None, 'grid'), may hold values from -0.5 to 0.5
- shocks: int32 [768, 2], P('groups'), parts along dimension 0, may hold values from 0 to 7
- shock_table: float32 [16, 2], P('groups'), parts along dimension 0, may hold values from -0.3 to 0.3
- first_weight: bfloat16 [131072, 2048], P(('groups', 'grid')), parts along dimension 0, may hold values from -0.03125 to 0.03125
- mid_weight: bfloat16 [4096, 2048], P('groups', 'grid'), parts along dimension 0, may hold values from -0.1875 to 0.1875
- head_weight: float32 [4096], P(('groups', 'grid')), parts along dimension 0, may hold values from -0.125 to 0.125
- cotangent: float32 [768], P('groups'), parts along dimension 0, may hold values from -6 to 6
Outputs:
- hist_next: float32 [768, 256, 256], P('groups', 'grid'), parts along dimension 0
- value: float32 [768], P('groups'), parts along dimension 0
- grad_first: bfloat16 [131072, 2048], P(('groups', 'grid')), parts along dimension 0
- grad_mid: bfloat16 [4096, 2048], P('groups', 'grid'), parts along dimension 0
- grad_head: float32 [4096], P(('groups', 'grid')), parts along dimension 0
There are 2 independent parts, one for each index of `groups`. A program takes and returns all parts, laid end to end along the dimension named above; an argument that names none is the same for every part. Nothing has to cross between parts.
All inputs are finite; a program needn't handle non-finite values.
Results may differ from a plain program's by a relative error of at most 0.0173.
Values may be sent and summed in bfloat16 or wider, within the bound.
A program may use at most 128 MiB of HBM per device.

v0:
```python
import jax
import jax.numpy as jnp
from jax import lax
from jax.sharding import PartitionSpec as P

diffusion_rate = 0.24


def padded_2(block, sides, width):
    for axis, dim in sides:
        count = lax.axis_size(axis)
        forward = [(i, i + 1) for i in range(count - 1)]
        backward = [(target, source) for source, target in forward]
        low = lax.ppermute(
            lax.slice_in_dim(block, block.shape[dim] - width, None, axis=dim), axis, forward
        )
        high = lax.ppermute(lax.slice_in_dim(block, 0, width, axis=dim), axis, backward)
        block = jnp.concatenate([low, block, high], axis=dim)
    return block


def column_shift(values, offset):
    zero_col = jnp.zeros_like(values[..., :1])
    if offset > 0:
        return jnp.concatenate([values[..., 1:], zero_col], axis=-1)
    return jnp.concatenate([zero_col, values[..., :-1]], axis=-1)


def shock_shift(levels_now, table):
    level_ids = lax.iota(jnp.int32, table.shape[0])
    onehot = (levels_now[:, None] == level_ids[None, :]).astype(jnp.float32)
    return jnp.sum(onehot[:, :, None] * table[None, :, :], axis=1)


def kfe_step(padded, drift_rows, shift_x, shift_y):
    velocity_x = drift_rows[0][None] + shift_x[:, None, None]
    velocity_y = drift_rows[1][1:-1][None] + shift_y[:, None, None]
    flux_x = velocity_x * padded
    centre = padded[:, 1:-1]
    flux_y = velocity_y * centre
    spread = (
        padded[:, 2:]
        + padded[:, :-2]
        + column_shift(centre, 1)
        + column_shift(centre, -1)
        - 4.0 * centre
    )
    carried = 0.5 * (flux_x[:, 2:] - flux_x[:, :-2]) + 0.5 * (
        column_shift(flux_y, 1) - column_shift(flux_y, -1)
    )
    return centre + diffusion_rate * spread - carried


def local(hist, drift, shocks, shock_table, first_weight, mid_weight, head_weight, cotangent):
    scenarios, row_count, columns = hist.shape
    step_count = shocks.shape[1]
    density = hist
    drift_ext = padded_2(drift, (("grid", 1),), 1)
    for section_no in range(step_count):
        shifts = shock_shift(shocks[:, section_no], shock_table)
        padded = padded_2(density, (("grid", 1),), 1)
        density = kfe_step(padded, drift_ext, shifts[:, 0], shifts[:, 1])
    inputs = density.astype(jnp.bfloat16).reshape(scenarios, row_count * columns)
    partial_first = jnp.dot(inputs, first_weight, preferred_element_type=jnp.float32)
    first_pre = lax.psum(partial_first, "grid")
    first_act = jnp.tanh(first_pre).astype(jnp.bfloat16)
    second_pre = jnp.dot(first_act, mid_weight, preferred_element_type=jnp.float32)
    second_act = jnp.tanh(second_pre).astype(jnp.bfloat16)
    second_f = second_act.astype(jnp.float32)
    value_part = jnp.dot(second_f, head_weight, precision=lax.Precision.HIGHEST)
    value = lax.psum(value_part, "grid")
    grad_head = jnp.dot(cotangent, second_f, precision=lax.Precision.HIGHEST)
    back_second = (cotangent[:, None] * head_weight[None, :] * (1.0 - second_f * second_f)).astype(
        jnp.bfloat16
    )
    grad_mid = lax.dot_general(
        first_act, back_second, (((0,), (0,)), ((), ())), preferred_element_type=jnp.float32
    )
    back_part = lax.dot_general(
        back_second, mid_weight, (((1,), (1,)), ((), ())), preferred_element_type=jnp.float32
    )
    back_raw = lax.psum(back_part, "grid")
    first_f = first_act.astype(jnp.float32)
    back_first = (back_raw * (1.0 - first_f * first_f)).astype(jnp.bfloat16)
    grad_first = lax.dot_general(
        inputs, back_first, (((0,), (0,)), ((), ())), preferred_element_type=jnp.float32
    )
    return (
        density,
        value,
        grad_first.astype(jnp.bfloat16),
        grad_mid.astype(jnp.bfloat16),
        grad_head,
    )


def solution(mesh):
    in_specs = (
        P("groups", "grid", None),
        P(None, "grid", None),
        P("groups", None),
        P("groups", None),
        P(("groups", "grid"), None),
        P("groups", "grid"),
        P(("groups", "grid")),
        P("groups"),
    )
    out_specs = (
        P("groups", "grid", None),
        P("groups"),
        P(("groups", "grid"), None),
        P("groups", "grid"),
        P(("groups", "grid")),
    )
    return jax.shard_map(local, mesh=mesh, in_specs=in_specs, out_specs=out_specs, check_vma=False)
```

profile of v0, /device:TPU:0, one launch (start us, length us, event | category | flops | bytes accessed | tf_op | source)
XLA Modules:
  0.0 387.2 jit_solution(2880481211151766229)
XLA Ops:
  7.2 0.0 copy-start
  7.2 0.0 all-reduce.11.cloned.1.call-start
  7.2 0.8 fusion.37
  8.0 2.4 collective-permute-start.2
  10.4 1.3 collective-permute-start.3
  11.7 3.4 fusion.35
  15.1 1.3 collective-permute-start
  16.4 0.8 copy.71
  17.2 6.7 %collective-permute-start.1 = (f32[384,1,256]{2,0,1:T(8,128)}, f32[384,1,256]{2,0,1:T(8,128)}, u32[]{:S(2)}, u32[]{:S(2)}) collective-permute-start(f32[384,1,256]{2,0,1:T(8,128)} %copy.71), channel_id=1, source_target_pairs={{0,1},{1,2},{2,3},{3,4},{4,5},{5,6},{6,7},{7,8},{8,9},{9,10},{10,1... | collective-permute-start | bytes 1179656 | tf_op jit(solution)/shard_map/ppermute | solution.py:14
  23.9 6.6 %copy.58 = f32[384,16,256]{0,2,1:T(8,128)} copy(f32[384,16,256]{2,1,0:T(8,128)} %param.8) | data formatting | bytes 12582912 | tf_op args[0]
  30.5 0.1 multiply_reduce_fusion
  30.7 10.8 %fusion.34 = (f32[384,16,255]{0,2,1:T(8,128)}, f32[384,16,255]{0,2,1:T(8,128)}) fusion(f32[384,16,256]{0,2,1:T(8,128)} %copy.58), kind=kLoop, calls=%fused_computation.63 | loop fusion | bytes 25067520 | tf_op jit(solution)/shard_map/slice | solution.py:25
  41.4 4.9 %add_multiply_fusion.1 = f32[384,16,256]{0,2,1:T(8,128)} fusion(f32[384,16,256]{0,2,1:T(8,128)} %copy.58, f32[384]{0:T(512)S(1)} %get-tuple-element.24, f32[16,256]{1,0:T(8,128)S(1)} %slice_bitcast_fusion), kind=kLoop, calls=%fused_computation.28 | loop fusion | flops 3145728 | bytes 12600832 | tf_op jit(solution)/shard_map/mul | solution.py:40
  46.4 10.8 %fusion.36 = (f32[384,16,255]{0,2,1:T(8,128)}, f32[384,16,255]{0,2,1:T(8,128)}) fusion(f32[384,16,256]{0,2,1:T(8,128)} %add_multiply_fusion.1), kind=kLoop, calls=%fused_computation.65 | loop fusion | bytes 25067520 | tf_op jit(solution)/shard_map/slice | solution.py:25
  57.2 0.0 slice-start
  57.2 0.2 copy.51
  57.4 1.3 copy.53
  58.7 6.0 %maximum_multiply_fusion = f32[384,18,256]{0,2,1:T(8,128)} fusion(f32[384,1,256]{0,2,1:T(8,128)S(1)} %copy.51, f32[384,16,256]{0,2,1:T(8,128)} %copy.58, f32[384,1,256]{0,2,1:T(8,128)S(1)} %copy.53, f32[384]{0:T(512)S(1)} %get-tuple-element.25, f32[18,256]{1,0:T(8,128)S(1)} %fusion.20), kind=kLoop, calls=%fused_computation.1 | loop fusion | flops 7077888 | bytes 14175744 | tf_op jit(solution)/shard_map/mul | solution.py:38
  64.8 2.4 slice-done.1
  67.2 14.2 %add_multiply_fusion = (f32[384,16,256]{0,2,1:T(8,128)}, f32[384,16,256]{0,2,1:T(8,128)S(1)}) fusion(f32[384]{0:T(512)S(1)} %get-tuple-element.20, f32[16,256]{1,0:T(8,128)S(1)} %slice_bitcast_fusion, f32[384,16,255]{0,2,1:T(8,128)} %get-tuple-element.43, f32[384,16,255]{0,2,1:T(8,128)} %get-tuple-element.42, f32[384,18,256]{0,2,1:T(8,128)} %maximum_multiply_fusion, ...), kind=kLoop, calls=%fused_computation.27 | loop fusion | flops 25165824 | bytes 57329152 | tf_op jit(solution)/shard_map/mul | solution.py:40
  81.4 2.6 copy-done.1
  84.0 0.1 fusion.32
  84.1 10.8 %fusion.31 = (f32[384,16,255]{0,2,1:T(8,128)}, f32[384,16,255]{0,2,1:T(8,128)}) fusion(f32[384,16,256]{0,2,1:T(8,128)} %copy-done.1), kind=kLoop, calls=%fused_computation.60 | loop fusion | bytes 25067520 | tf_op jit(solution)/shard_map/slice | solution.py:25
  94.9 0.2 copy.63
  95.1 1.3 collective-permute-start.4
  96.4 0.2 copy.65
  96.5 4.3 %collective-permute-start.5 = (f32[384,1,256]{2,0,1:T(8,128)S(1)}, f32[384,1,256]{2,0,1:T(8,128)}, u32[]{:S(2)}, u32[]{:S(2)}) collective-permute-start(f32[384,1,256]{2,0,1:T(8,128)S(1)} %copy.65), channel_id=1, source_target_pairs={{0,1},{1,2},{2,3},{3,4},{4,5},{5,6},{6,7},{7,8},{8,9},{9,10},{10,1... | collective-permute-start | bytes 1179656 | tf_op jit(solution)/shard_map/ppermute | solution.py:14
  100.8 10.7 %fusion.33 = (f32[384,16,255]{0,2,1:T(8,128)}, f32[384,16,255]{0,2,1:T(8,128)}) fusion(f32[384,16,256]{0,2,1:T(8,128)} %get-tuple-element.30), kind=kLoop, calls=%fused_computation.62 | loop fusion | bytes 25067520 | tf_op jit(solution)/shard_map/slice | solution.py:25
  111.5 0.2 copy.64
  111.7 1.3 copy.66
  113.1 5.5 %maximum_multiply_fusion.1 = f32[384,18,256]{0,2,1:T(8,128)} fusion(f32[384,1,256]{0,2,1:T(8,128)S(1)} %copy.64, f32[384,16,256]{0,2,1:T(8,128)} %copy-done.1, f32[384,1,256]{0,2,1:T(8,128)S(1)} %copy.66, f32[384]{0:T(512)S(1)} %get-tuple-element.21, f32[18,256]{1,0:T(8,128)S(1)} %fusion.20), kind=kLoop, calls=%fused_computation.2 | loop fusion | flops 7077888 | bytes 14175744 | tf_op jit(solution)/shard_map/mul | solution.py:38
  118.6 0.1 slice-done.3
  118.7 17.3 %fusion.28 = (bf16[384,16,256]{0,2,1:T(8,128)(2,1)S(1)}, f32[384,16,256]{0,2,1:T(8,128)}) fusion(f32[384,16,255]{0,2,1:T(8,128)} %get-tuple-element.37, f32[384,16,255]{0,2,1:T(8,128)} %get-tuple-element.36, f32[384,18,256]{0,2,1:T(8,128)} %maximum_multiply_fusion.1, f32[384,16,256]{0,2,1:T(8,128)S(1)} %bitcast.21, f32[384,16,255]{0,2,1:T(8,128)} %get-tuple-element.33, ...), kind=kLoop, calls=%fused_computation.59 | loop fusion | flops 23592960 | bytes 54165504 | tf_op jit(solution)/shard_map/convert_element_type | solution.py:63
  136.0 1.7 copy-done.3
  137.7 12.1 %fusion.38 = f32[384,2048]{1,0:T(8,128)} fusion(bf16[384,4096]{0,1:T(8,128)(2,1)S(1)} %bitcast.22, bf16[4096,2048]{1,0:T(8,128)(2,1)} %param.12), kind=kOutput, calls=%fused_computation.67 | convolution fusion | flops 6442450944 | bytes 23068672 | tf_op jit(solution)/shard_map/dot_general | solution.py:64
  149.8 0.0 all-reduce.11.cloned.1.call-update
  149.8 0.0 all-reduce.13.cloned.1.call-start
  149.9 106.9 %all-reduce.11.cloned.1.call-done = f32[384,2048]{1,0:T(8,128)} async-done(((f32[384,2048]{1,0:T(8,128)}), f32[384,2048]{1,0:T(8,128)}) %all-reduce.11.cloned.1.call-update) | async-done | bytes 3145744 | tf_op jit(solution)/shard_map/psum | solution.py:65
  256.7 2.5 fusion.19
  259.2 2.3 fusion.23
  261.5 0.0 all-reduce.13.cloned.1.call-update
  261.6 6.7 %copy.69 = f32[384,16,256]{2,1,0:T(8,128)} copy(f32[384,16,256]{0,2,1:T(8,128)} %get-tuple-element.29) | data formatting | bytes 12582912
  268.3 0.2 convolution_reduce_fusion
  268.5 31.0 %psum.22 = f32[384]{0:T(512)} all-reduce(f32[384]{0:T(512)S(1)} %convolution_reduce_fusion), channel_id=1, replica_groups=mesh['groups'=2,'grid'=16] {'grid'}, use_global_device_ids=true, to_apply=%region_3.0 | all-reduce | flops 384 | bytes 3072 | tf_op jit(solution)/shard_map/psum | solution.py:71
  299.6 0.7 convolution_bitcast_fusion
  300.2 3.4 convolution_convert_fusion.1
  303.6 61.2 %all-reduce.13.cloned.1.call-done = f32[384,2048]{1,0:T(8,128)} async-done(((f32[384,2048]{1,0:T(8,128)}), f32[384,2048]{1,0:T(8,128)}) %all-reduce.13.cloned.1.call-update) | async-done | bytes 3145744 | tf_op jit(solution)/shard_map/psum | solution.py:82
  364.9 15.5 %convolution_convert_fusion = bf16[4096,2048]{1,0:T(8,128)(2,1)} fusion(bf16[384,4096]{0,1:T(8,128)(2,1)} %bitcast.23, f32[384,2048]{1,0:T(8,128)} %all-reduce.13.cloned.1.call-done, f32[384,2048]{1,0:T(8,128)} %all-reduce.11.cloned.1.call-done), kind=kOutput, calls=%fused_computation | convolution fusion | flops 6455558144 | bytes 26214400 | tf_op jit(solution)/shard_map/dot_general | solution.py:85
  (36 shorter events, 0.2 us)
Async XLA Ops:
  7.2 249.6 %copy-start = (bf16[2048,128]{1,0:T(8,128)(2,1)S(1)}, bf16[2048,128]{1,0:T(8,128)(2,1)}, u32[]{:S(2)}) copy-start(bf16[2048,128]{1,0:T(8,128)(2,1)} %param.13) | copy-start | bytes 1572868
  7.2 249.6 %all-reduce.11.cloned.1.call-start = ((), (), s32[]{:S(2)}) async-start(), calls=%async_computation | async-start | bytes 6291456 | tf_op jit(solution)/shard_map/psum | solution.py:65
  8.0 49.2 %collective-permute-start.2 = (f32[2,1,256]{2,1,0:T(1,128)S(1)}, f32[2,1,256]{2,1,0:T(1,128)S(1)}, u32[]{:S(2)}, u32[]{:S(2)}) collective-permute-start(f32[2,1,256]{2,1,0:T(1,128)S(1)} %get-tuple-element.44), channel_id=1, source_target_pairs={{0,1},{1,2},{2,3},{3,4},{4,5},{5,6},{6,7},{7,8},{8,9},{9,10},{10,1... | collective-permute-start | bytes 6152 | tf_op jit(solution)/shard_map/ppermute | solution.py:14
  10.4 46.8 %collective-permute-start.3 = (f32[2,1,256]{2,1,0:T(1,128)S(1)}, f32[2,1,256]{2,1,0:T(1,128)S(1)}, u32[]{:S(2)}, u32[]{:S(2)}) collective-permute-start(f32[2,1,256]{2,1,0:T(1,128)S(1)} %get-tuple-element.45), channel_id=1, source_target_pairs={{1,0},{2,1},{3,2},{4,3},{5,4},{6,5},{7,6},{8,7},{9,8},{10,9},{11,1... | collective-permute-start | bytes 6152 | tf_op jit(solution)/shard_map/ppermute | solution.py:17
  15.1 42.1 %collective-permute-start = (f32[384,1,256]{2,0,1:T(8,128)S(1)}, f32[384,1,256]{2,0,1:T(8,128)S(1)}, u32[]{:S(2)}, u32[]{:S(2)}) collective-permute-start(f32[384,1,256]{2,0,1:T(8,128)S(1)} %copy.70), channel_id=1, source_target_pairs={{1,0},{2,1},{3,2},{4,3},{5,4},{6,5},{7,6},{8,7},{9,8},{10,9},{11,1... | collective-permute-start | bytes 1179656 | tf_op jit(solution)/shard_map/ppermute | solution.py:17
  17.2 13.3 %copy-start.4 = (f32[2,16,256]{2,1,0:T(8,128)S(1)}, f32[2,16,256]{2,1,0:T(8,128)}, u32[]{:S(2)}) copy-start(f32[2,16,256]{2,1,0:T(8,128)} %param.9) | copy-start | bytes 98308
  17.2 13.3 %copy-start.7 = (s32[384,2]{0,1:T(2,128)S(1)}, s32[384,2]{0,1:T(2,128)}, u32[]{:S(2)}) copy-start(s32[384,2]{0,1:T(2,128)} %param.10) | copy-start | bytes 9220
  17.2 13.3 %copy-start.8 = (f32[8,2]{0,1:T(2,128)S(1)}, f32[8,2]{0,1:T(2,128)}, u32[]{:S(2)}) copy-start(f32[8,2]{0,1:T(2,128)} %param.11) | copy-start | bytes 196
  17.2 40.2 %collective-permute-start.1 = (f32[384,1,256]{2,0,1:T(8,128)}, f32[384,1,256]{2,0,1:T(8,128)}, u32[]{:S(2)}, u32[]{:S(2)}) collective-permute-start(f32[384,1,256]{2,0,1:T(8,128)} %copy.71), channel_id=1, source_target_pairs={{0,1},{1,2},{2,3},{3,4},{4,5},{5,6},{6,7},{7,8},{8,9},{9,10},{10,1... | collective-permute-start | bytes 1179656 | tf_op jit(solution)/shard_map/ppermute | solution.py:14
  57.2 7.5 %slice-start = ((s8[6291456]{0:T(1024)(128)(4,1)}), s8[2097152]{0:T(1024)(128)(4,1)S(1)}, s32[]{:S(2)}) async-start(s8[6291456]{0:T(1024)(128)(4,1)} %bitcast.18), calls=%async_computation.2 | async-start | bytes 4194304
  58.7 8.5 %slice-start.1 = ((s8[6291456]{0:T(1024)(128)(4,1)}), s8[4194304]{0:T(1024)(128)(4,1)S(1)}, s32[]{:S(2)}) async-start(s8[6291456]{0:T(1024)(128)(4,1)} %bitcast.18), calls=%async_computation.3 | async-start | bytes 8388608
  58.7 8.5 %copy-start.2 = (f32[384,16,255]{0,2,1:T(8,128)S(1)}, f32[384,16,255]{0,2,1:T(8,128)}, u32[]{:S(2)}) copy-start(f32[384,16,255]{0,2,1:T(8,128)} %get-tuple-element.38) | copy-start | bytes 18800644
  81.4 2.6 copy-start.1
  95.1 16.5 %collective-permute-start.4 = (f32[384,1,256]{2,0,1:T(8,128)S(1)}, f32[384,1,256]{2,0,1:T(8,128)S(1)}, u32[]{:S(2)}, u32[]{:S(2)}) collective-permute-start(f32[384,1,256]{2,0,1:T(8,128)S(1)} %copy.63), channel_id=1, source_target_pairs={{1,0},{2,1},{3,2},{4,3},{5,4},{6,5},{7,6},{8,7},{9,8},{10,9},{11,1... | collective-permute-start | bytes 1179656 | tf_op jit(solution)/shard_map/ppermute | solution.py:17
  96.5 15.2 %collective-permute-start.5 = (f32[384,1,256]{2,0,1:T(8,128)S(1)}, f32[384,1,256]{2,0,1:T(8,128)}, u32[]{:S(2)}, u32[]{:S(2)}) collective-permute-start(f32[384,1,256]{2,0,1:T(8,128)S(1)} %copy.65), channel_id=1, source_target_pairs={{0,1},{1,2},{2,3},{3,4},{4,5},{5,6},{6,7},{7,8},{8,9},{9,10},{10,1... | collective-permute-start | bytes 1179656 | tf_op jit(solution)/shard_map/ppermute | solution.py:14
  111.7 6.9 %slice-start.2 = ((s8[6291456]{0:T(1024)(128)(4,1)}), s8[2097152]{0:T(1024)(128)(4,1)S(1)}, s32[]{:S(2)}) async-start(s8[6291456]{0:T(1024)(128)(4,1)} %bitcast.20), calls=%async_computation.4 | async-start | bytes 4194304
  113.0 5.7 %slice-start.3 = ((s8[6291456]{0:T(1024)(128)(4,1)}), s8[4194304]{0:T(1024)(128)(4,1)S(1)}, s32[]{:S(2)}) async-start(s8[6291456]{0:T(1024)(128)(4,1)} %bitcast.20), calls=%async_computation.5 | async-start | bytes 8388608
  136.0 1.7 copy-start.3
  149.8 109.4 %copy-start.5 = (f32[384]{0:T(512)S(1)}, f32[384]{0:T(512)}, u32[]{:S(2)}) copy-start(f32[384]{0:T(512)} %param.15) | copy-start | bytes 4612
  149.8 109.4 %copy-start.6 = (f32[128]{0:T(128)S(1)}, f32[128]{0:T(128)}, u32[]{:S(2)}) copy-start(f32[128]{0:T(128)} %param.14) | copy-start | bytes 1540
  149.8 215.0 %all-reduce.13.cloned.1.call-start = ((), (), s32[]{:S(2)}) async-start(), calls=%async_computation.1 | async-start | bytes 6291456 | tf_op jit(solution)/shard_map/psum | solution.py:82
Sparse Core Ops, SparseCore 0:
  150.0 106.7 all-reduce.10
  261.7 103.1 all-reduce.12
where the time goes:
time: 388 us; the launch traced here: 387 us
  waiting for transfers between devices  168 us (43%)
  local copies, waits for them, and re-layouts  71.6 us (18%)
  other arithmetic  48.1 us (12%)
  matrix products  36.7 us (9%)
  blocking collectives  31 us (8%)
  starting transfers between devices  17.3 us (4%)
  between operations  14.3 us (4%)
    psum x1, waiting for transfers between devices, local(): first_pre = lax.psum(partial_first, 'grid')  107 us
    psum x1, waiting for transfers between devices, local(): back_raw = lax.psum(back_part, 'grid')  61.2 us
    slice x4, local copies, waits for them, and re-layouts, column_shift(): return jnp.concatenate([values[..., 1:], zero_col], axis=-1)  43.1 us
    psum x1, blocking collectives, local(): value = lax.psum(value_part, 'grid')  31 us
    unnamed x31, local copies, waits for them, and re-layouts  21 us
    mul x2, other arithmetic, kfe_step(): flux_y = velocity_y * centre  19.2 us
    convert_element_type x1, other arithmetic, local(): density.astype(jnp.bfloat16).reshape(scenarios, row_count * columns)  17.3 us
    dot_general x1, matrix products, local(): lax.dot_general(inputs, back_first, (((0,), (0,)), ((), ())), preferred_e...  15.5 us
  transfers between devices with their start and end apart: 8, of which 2 were waited for; matrix products, arithmetic and copies ran while one was open for 15% of the time, Pallas kernels for 0%

commit v1 on v0

v1 whole, which is shorter than its diff:
```python
import functools
import jax
import jax.numpy as jnp
from jax import lax
from jax.experimental import pallas as pl
from jax.experimental.pallas import tpu as pltpu
from jax.sharding import PartitionSpec as P

diffusion_rate = 0.24
F32, BF16 = jnp.float32, jnp.bfloat16
VMEM = pl.BlockSpec(memory_space=pltpu.VMEM)
SMEM = pl.BlockSpec(memory_space=pltpu.SMEM)
MESH = pl.DeviceIdType.MESH


def remote(src, dst, send, recv, target):
    return pltpu.make_async_remote_copy(
        src_ref=src,
        dst_ref=dst,
        send_sem=send,
        recv_sem=recv,
        device_id={"grid": target},
        device_id_type=MESH,
    )


def halo_kernel(n, rows, lanes, *refs):
    x_refs, refs = refs[:lanes], refs[lanes:]
    drift_ref, lo_ref, hi_ref, dlo_ref, dhi_ref, up, down, send, recv = refs
    me = lax.axis_index("grid")
    count = up.shape[1]
    barrier = pltpu.get_barrier_semaphore()
    has_next, has_prev = me < n - 1, me > 0

    @pl.when(has_next)
    def _():
        pl.semaphore_signal(barrier, inc=1, device_id={"grid": me + 1}, device_id_type=MESH)

    @pl.when(has_prev)
    def _():
        pl.semaphore_signal(barrier, inc=1, device_id={"grid": me - 1}, device_id_type=MESH)

    @pl.when(has_next)
    def _():
        for i in range(2):
            for k in range(lanes):
                edge = x_refs[k][pl.ds(rows - 2 + i, count, stride=rows), :]
                up[i, :, k * 128 : (k + 1) * 128] = edge.astype(BF16)

    @pl.when(has_prev)
    def _():
        for i in range(2):
            for k in range(lanes):
                edge = x_refs[k][pl.ds(i, count, stride=rows), :]
                down[i, :, k * 128 : (k + 1) * 128] = edge.astype(BF16)

    pl.semaphore_wait(barrier, has_next.astype(jnp.int32) + has_prev.astype(jnp.int32))

    def upward():
        return (
            remote(up, lo_ref, send.at[0], recv.at[0], me + 1),
            remote(drift_ref, dlo_ref, send.at[1], recv.at[1], me + 1),
        )

    def downward():
        return (
            remote(down, hi_ref, send.at[2], recv.at[2], me - 1),
            remote(drift_ref, dhi_ref, send.at[3], recv.at[3], me - 1),
        )

    @pl.when(has_next)
    def _():
        for copy in upward():
            copy.start()

    @pl.when(has_prev)
    def _():
        for copy in downward():
            copy.start()

    @pl.when(jnp.logical_not(has_next))
    def _():
        hi_ref[...] = jnp.zeros_like(hi_ref)
        dhi_ref[...] = jnp.zeros_like(dhi_ref)

    @pl.when(jnp.logical_not(has_prev))
    def _():
        lo_ref[...] = jnp.zeros_like(lo_ref)
        dlo_ref[...] = jnp.zeros_like(dlo_ref)

    @pl.when(has_next)
    def _():
        for copy in upward():
            copy.wait_send()
        for copy in downward():
            copy.wait_recv()

    @pl.when(has_prev)
    def _():
        for copy in downward():
            copy.wait_send()
        for copy in upward():
            copy.wait_recv()


def halo(n, rows, x2, drift2):
    count, columns = x2.shape[0] // rows, x2.shape[1]
    edge = jax.ShapeDtypeStruct((2, count, columns), BF16)
    side = jax.ShapeDtypeStruct(drift2.shape, F32)
    lanes = columns // 128
    strips = [
        pl.BlockSpec((x2.shape[0], 128), functools.partial(lambda k, i: (0, k), k))
        for k in range(lanes)
    ]
    return pl.pallas_call(
        functools.partial(halo_kernel, n, rows, lanes),
        grid=(1,),
        out_shape=(edge, edge, side, side),
        in_specs=strips + [VMEM],
        out_specs=(VMEM,) * 4,
        scratch_shapes=[
            pltpu.VMEM(edge.shape, BF16),
            pltpu.VMEM(edge.shape, BF16),
            pltpu.SemaphoreType.DMA((4,)),
            pltpu.SemaphoreType.DMA((4,)),
        ],
        compiler_params=pltpu.CompilerParams(
            collective_id=0, has_side_effects=True, vmem_limit_bytes=48 << 20
        ),
    )(*[x2] * lanes, drift2)


def stencil_kernel(
    n, rows, extended, steps, shocks, table, x_ref, lo_ref, hi_ref, drift_ref, dlo_ref, dhi_ref,
    out_ref, flat_ref, coef, *strips
):
    block = lo_ref.shape[1]
    columns = x_ref.shape[1]
    stored = x_ref.shape[0] // block
    extra = extended - stored
    filler = extended - rows - 4
    lanes = columns // 128
    halo_rows, plain = strips[:lanes], strips[lanes:]
    me = lax.axis_index("grid")
    first_no = pl.program_id(0) * block
    lane = lax.broadcasted_iota(jnp.int32, (1, columns), 1)
    not_first = (lane > 0).astype(F32)
    not_last = (lane < columns - 1).astype(F32)

    @pl.when(pl.program_id(0) == 0)
    def _():
        for part in range(2):
            base = part * rows
            pieces = [drift_ref[pl.ds(base, rows), :], dhi_ref[pl.ds(base, 2), :]]
            if filler > 0:
                pieces.append(jnp.zeros((filler, columns), F32))
            pieces.append(dlo_ref[pl.ds(base + rows - 2, 2), :])
            whole = 0.5 * jnp.concatenate(pieces, axis=0)
            before, after = diffusion_rate - whole, diffusion_rate + whole
            if part == 1:
                before, after = before * not_first, after * not_last
            coef[2 * part] = before
            coef[2 * part + 1] = after
        for strip in halo_rows:
            strip[...] = jnp.zeros_like(strip)

    for k in range(lanes if extra else 0):
        part = slice(k * 128, (k + 1) * 128)
        for i in range(2):
            halo_rows[k][pl.ds(i, block, stride=extra), :] = hi_ref[i, :, part].astype(F32)
            halo_rows[k][pl.ds(extra - 2 + i, block, stride=extra), :] = lo_ref[
                i, :, part
            ].astype(F32)

    row = lax.broadcasted_iota(jnp.int32, (extended, columns), 0)
    outside = ((row >= rows) & (row < rows + 2) & (me == n - 1)) | (
        (row >= extended - 2) & (me == 0)
    )

    def one(s, carry):
        c = x_ref[pl.ds(pl.multiple_of(s * stored, 8), stored), :]
        if extra:
            at = pl.ds(pl.multiple_of(s * extra, 8), extra)
            ends = jnp.concatenate([strip[at, :] for strip in halo_rows], axis=1)
            c = jnp.concatenate([c, ends], axis=0)
        for t in range(steps):
            level = shocks[(first_no + s) * steps + t]
            half_x, half_y = 0.5 * table[2 * level], 0.5 * table[2 * level + 1]
            above = (coef[0] - half_x) * c
            below = (coef[1] + half_x) * c
            left = (coef[2] - half_y * not_first) * c
            right = (coef[3] + half_y * not_last) * c
            c = (
                (1.0 - 4.0 * diffusion_rate) * c
                + (pltpu.roll(above, extended - 1, 0) + pltpu.roll(below, 1, 0))
                + (pltpu.roll(left, columns - 1, 1) + pltpu.roll(right, 1, 1))
            )
            if t < steps - 1:
                c = jnp.where(outside, 0.0, c)
        at = pl.ds(pl.multiple_of(s * stored, 8), stored)
        out_ref[at, :] = c[:stored]
        for k in range(lanes):
            plain[k][at, :] = c[:stored, k * 128 : (k + 1) * 128]
        return carry

    lax.fori_loop(0, block, one, 0, unroll=4)
    for r in range(rows):
        for k in range(lanes):
            at = r * columns + k * 128
            row_now = plain[k][pl.ds(r, block, stride=stored), :]
            flat_ref[:, at : at + 128] = row_now.astype(BF16)


def stencil(n, rows, steps, shocks, table, x2, lo, hi, drift2, dlo, dhi):
    columns = x2.shape[1]
    count = x2.shape[0] // rows
    extended = -(-(rows + 4) // 8) * 8
    stored = rows
    if rows % 8:
        stored = extended
        before, after = [jnp.swapaxes(edge, 0, 1).astype(F32) for edge in (lo, hi)]
        filler = jnp.zeros((count, extended - rows - 4, columns), F32)
        x3 = x2.reshape(count, rows, columns)
        x2 = jnp.concatenate([x3, after, filler, before], axis=1).reshape(-1, columns)
    block = max(b for b in (8, 16, 32) if count % b == 0)
    whole = pl.BlockSpec(drift2.shape, lambda i: (0, 0))
    edge = pl.BlockSpec((2, block, columns), lambda i: (0, i, 0))
    cells = pl.BlockSpec((block * stored, columns), lambda i: (i, 0))
    density, flat = pl.pallas_call(
        functools.partial(stencil_kernel, n, rows, extended, steps),
        grid=(count // block,),
        out_shape=(
            jax.ShapeDtypeStruct(x2.shape, F32),
            jax.ShapeDtypeStruct((count, rows * columns), BF16),
        ),
        in_specs=[SMEM, SMEM, cells, edge, edge, whole, whole, whole],
        out_specs=(cells, pl.BlockSpec((block, rows * columns), lambda i: (i, 0))),
        scratch_shapes=[
            pltpu.VMEM((4, extended, columns), F32),
        ]
        + [pltpu.VMEM((block * max(extended - stored, 8), 128), F32)] * (columns // 128)
        + [pltpu.VMEM((block * stored, 128), F32)] * (columns // 128),
    )(shocks, table, x2, lo, hi, drift2, dlo, dhi)
    return density.reshape(count, stored, columns)[:, :rows], flat


def halvings(rows, columns, count):
    plan = []
    for _ in range(count):
        if columns >= 256:
            columns //= 2
            plan.append((1, rows, columns))
        else:
            rows //= 2
            plan.append((0, rows, columns))
    return plan


def reduce_kernel(n, plan, orders, wide, second_pass, *refs):
    stages = len(plan)
    refs = list(refs)
    x_ref = refs.pop(0)
    if second_pass:
        first_ref, v_ref = refs.pop(0), refs.pop(0)
    out_ref = refs.pop(0)
    if second_pass:
        v_out = refs.pop(0)
    streams = len(orders)
    got = [[refs.pop(0) for _ in range(stages)] for _ in range(streams)]
    acc = [[refs.pop(0) for _ in range(stages - 1)] + [None] for _ in range(streams)]
    narrow = [[None] * wide + [refs.pop(0) for _ in range(wide, stages)] for _ in range(streams)]
    if second_pass:
        v_got, v_acc = refs.pop(0), refs.pop(0)
        v_send, v_recv = refs.pop(0), refs.pop(0)
    send, recv = refs

    me = lax.axis_index("grid")
    bits = [lax.rem(me // (1 << b), 2) for b in range(stages)]
    partner = [me + (1 << b) * (1 - 2 * bits[b]) for b in range(stages)]
    height = x_ref.shape[0] // streams

    barrier = pltpu.get_barrier_semaphore()
    for b in range(stages):
        pl.semaphore_signal(barrier, inc=1, device_id={"grid": partner[b]}, device_id_type=MESH)
    pl.semaphore_wait(barrier, stages)

    place = []
    for t in range(streams):
        row, col = t * height, 0
        spots = []
        for s in range(stages):
            dim, r, c = plan[s]
            bit = bits[orders[t][s]]
            if dim == 1:
                col = pl.multiple_of(col + bit * c, 128)
            else:
                row = pl.multiple_of(row + bit * r, 16)
            spots.append((pl.ds(row, r), pl.ds(col, c)))
        place.append(spots)

    def half(t, s, which):
        dim, r, c = plan[s]
        at_row, at_col = (t * height if s == 0 else 0), 0
        if dim == 1:
            at_col = pl.multiple_of(which * c, 128)
        else:
            at_row = pl.multiple_of(at_row + which * r, 16)
        return (x_ref if s == 0 else acc[t][s - 1]), (pl.ds(at_row, r), pl.ds(at_col, c))

    def scatter(t, s):
        b = orders[t][s]
        ref, spot = half(t, s, 1 - bits[b])
        sem = t * 2 * stages + s
        src = ref.at[spot] if s < wide else narrow[t][s]
        return remote(src, got[t][s], send.at[sem], recv.at[sem], partner[b])

    def begin(t, s):
        if s >= wide:
            ref, spot = half(t, s, 1 - bits[orders[t][s]])
            narrow[t][s][...] = ref[spot].astype(BF16)
        scatter(t, s).start()

    def gather(t, s):
        b = orders[t][s]
        sem = t * 2 * stages + stages + s
        spot = out_ref.at[place[t][s]]
        return remote(spot, spot, send.at[sem], recv.at[sem], partner[b])

    def sum_values(s):
        src = v_ref if s == 0 else v_acc.at[s - 1]
        return remote(src, v_got.at[s], v_send.at[s], v_recv.at[s], partner[s])

    for t in range(streams):
        begin(t, 0)
    if second_pass:
        sum_values(0).start()
    for s in range(stages):
        for t in range(streams):
            scatter(t, s).wait_recv()
            ref, spot = half(t, s, bits[orders[t][s]])
            total = ref[spot] + got[t][s][...].astype(F32)
            if s < stages - 1:
                acc[t][s][...] = total
                begin(t, s + 1)
            else:
                if second_pass:
                    first = first_ref[place[t][s]].astype(F32)
                    total = total * (1.0 - first * first)
                else:
                    total = jnp.tanh(total)
                out_ref[place[t][s]] = total.astype(BF16)
                gather(t, s).start()
        if second_pass:
            sum_values(s).wait_recv()
            mine = v_ref[...] if s == 0 else v_acc[s - 1]
            if s < stages - 1:
                v_acc[s] = mine + v_got[s]
                sum_values(s + 1).start()
            else:
                v_out[...] = mine + v_got[s]
    for s in reversed(range(stages)):
        for t in range(streams):
            gather(t, s).wait_recv()
            if s > 0:
                gather(t, s - 1).start()
    for s in range(stages):
        for t in range(streams):
            scatter(t, s).wait_send()
            gather(t, s).wait_send()
        if second_pass:
            sum_values(s).wait_send()


def reduce_gather(n, x, wide, first=None, v=None):
    stages = n.bit_length() - 1
    assert n == 1 << stages
    streams = 2
    plan = halvings(x.shape[0] // streams, x.shape[1], stages)
    orders = [list(range(stages)), list(range(stages))]
    if stages > 2:
        orders[1][1:3] = [2, 1]
    second_pass = first is not None
    out_shape = [jax.ShapeDtypeStruct(x.shape, BF16)]
    operands = [x]
    if second_pass:
        out_shape.append(jax.ShapeDtypeStruct(v.shape, F32))
        operands += [first, v]
    wide = min(wide, stages)
    scratch = [
        pltpu.VMEM(p[1:], F32 if s < wide else BF16)
        for _ in range(streams)
        for s, p in enumerate(plan)
    ]
    scratch += [pltpu.VMEM(p[1:], F32) for _ in range(streams) for p in plan[:-1]]
    scratch += [pltpu.VMEM(p[1:], BF16) for _ in range(streams) for p in plan[wide:]]
    if second_pass:
        scratch += [pltpu.VMEM((stages,) + v.shape, F32)] * 2
        scratch += [pltpu.SemaphoreType.DMA((stages,))] * 2
    scratch += [pltpu.SemaphoreType.DMA((2 * streams * stages,))] * 2
    return pl.pallas_call(
        functools.partial(reduce_kernel, n, plan, orders, wide, second_pass),
        out_shape=tuple(out_shape),
        in_specs=[VMEM] * len(operands),
        out_specs=(VMEM,) * len(out_shape),
        scratch_shapes=scratch,
        compiler_params=pltpu.CompilerParams(
            collective_id=2 if second_pass else 1,
            has_side_effects=True,
            vmem_limit_bytes=48 << 20,
        ),
    )(*operands)


def local(n, hist, drift, shocks, shock_table, first_weight, mid_weight, head_weight, cotangent):
    scenarios, row_count, columns = hist.shape
    x2 = hist.reshape(scenarios * row_count, columns)
    drift2 = drift.reshape(2 * row_count, columns)
    lo, hi, dlo, dhi = halo(n, row_count, x2, drift2)
    density, inputs = stencil(
        n, row_count, shocks.shape[1], shocks.reshape(-1), shock_table.reshape(-1),
        x2, lo, hi, drift2, dlo, dhi,
    )
    partial_first = jnp.dot(inputs, first_weight, preferred_element_type=F32)
    (first_act,) = reduce_gather(n, partial_first, 2)
    second_pre = jnp.dot(first_act, mid_weight, preferred_element_type=F32)
    second_act = jnp.tanh(second_pre).astype(BF16)
    second_f = second_act.astype(F32)
    head_rows = jnp.broadcast_to(head_weight[None, :], (8, head_weight.shape[0]))
    value_part = lax.dot_general(
        head_rows, second_f, (((1,), (1,)), ((), ())), precision=lax.Precision.HIGHEST
    )
    grad_head = jnp.dot(cotangent, second_f, precision=lax.Precision.HIGHEST)
    back_second = (cotangent[:, None] * head_weight[None, :] * (1.0 - second_f * second_f)).astype(
        BF16
    )
    back_part = lax.dot_general(
        back_second, mid_weight, (((1,), (1,)), ((), ())), preferred_element_type=F32
    )
    back_first, value = reduce_gather(n, back_part, 1, first_act, value_part)
    grad_mid = lax.dot_general(
        first_act, back_second, (((0,), (0,)), ((), ())), preferred_element_type=F32
    )
    grad_first = lax.dot_general(
        inputs, back_first, (((0,), (0,)), ((), ())), preferred_element_type=F32
    )
    return (
        density,
        value[0],
        grad_first.astype(BF16),
        grad_mid.astype(BF16),
        grad_head,
    )


def solution(mesh):
    in_specs = (
        P("groups", "grid", None),
        P(None, "grid", None),
        P("groups", None),
        P("groups", None),
        P(("groups", "grid"), None),
        P("groups", "grid"),
        P(("groups", "grid")),
        P("groups"),
    )
    out_specs = (
        P("groups", "grid", None),
        P("groups"),
        P(("groups", "grid"), None),
        P("groups", "grid"),
        P(("groups", "grid")),
    )
    return jax.shard_map(
        functools.partial(local, mesh.shape["grid"]),
        mesh=mesh,
        in_specs=in_specs,
        out_specs=out_specs,
        check_vma=False,
    )
```

time: 388 us -> 157 us (0.40)
  waiting for transfers between devices: 168 us -> 0 us
  Pallas kernels: 0 us -> 120 us
  local copies, waits for them, and re-layouts: 71.6 us -> 7.69 us
  other arithmetic: 48.1 us -> 0 us
  blocking collectives: 31 us -> 0 us
  starting transfers between devices: 17.3 us -> 0 us
  between operations: 14.3 us -> 0.73 us
  matrix products: 36.7 us -> 28.9 us
    psum x2 -> x0, waiting for transfers between devices: 168 us -> none  [the longest x1 107 us: local(): first_pre = lax.psum(partial_first, 'grid')]
    pallas_call x0 -> x4, Pallas kernels: none -> 120 us  [the longest x2 88.3 us: reduce_gather(): pl.pallas_call(functools.partial(reduce_kernel, n, plan, orders, wide, se...]
    slice x12 -> x1, local copies, waits for them, and re-layouts: 47.7 us -> 0.6 us  [local(): value[0]]
    psum x1 -> x0, blocking collectives: 31 us -> none  [local(): value = lax.psum(value_part, 'grid')]
    mul x4 -> x0, other arithmetic: 30.7 us -> none  [the longest x2 19.2 us: kfe_step(): flux_y = velocity_y * centre]
    convert_element_type x2 -> x0, other arithmetic: 17.3 us -> none  [the longest x1 17.3 us: local(): density.astype(jnp.bfloat16).reshape(scenarios, row_count * columns)]
    ppermute x6 -> x0, starting transfers between devices: 17.2 us -> none  [the longest x3 13.3 us: padded_2(): lax.ppermute(lax.slice_in_dim(block, block.shape[dim] - width, None, axis...]
    unnamed x31 -> x21, local copies, waits for them, and re-layouts: 21 us -> 5.77 us
  transfers between devices with their start and end apart: 8 -> 0, of which waited for: 2 -> 0; matrix products, arithmetic and copies ran while one was open for 15% -> 0% of each run, Pallas kernels for 0% -> 0%
where the time goes in v1:
time: 157 us
  Pallas kernels  120 us (76%)
  matrix products  28.9 us (18%)
  local copies, waits for them, and re-layouts  7.69 us (5%)
    pallas_call x2, Pallas kernels, reduce_gather(): pl.pallas_call(functools.partial(reduce_kernel, n, plan, orders, wide, se...  88.3 us
    pallas_call x1, Pallas kernels, stencil(): pl.pallas_call(functools.partial(stencil_kernel, n, rows, extended, steps...  24.1 us
    dot_general x1, matrix products, local(): lax.dot_general(inputs, back_first, (((0,), (0,)), ((), ())), preferred_e...  12.6 us
    dot_general x1, matrix products, local(): partial_first = jnp.dot(inputs, first_weight, preferred_element_type=F32)  11.1 us
    pallas_call x1, Pallas kernels, halo(): pl.pallas_call(functools.partial(halo_kernel, n, rows, lanes), grid=(1,),...  7.29 us
    unnamed x21, local copies, waits for them, and re-layouts  5.77 us

profile of v1, /device:TPU:0, one launch (start us, length us, event | category | flops | bytes accessed | tf_op | source)
XLA Modules:
  0.0 157.1 jit_solution(17911994817791888243)
XLA Ops:
  0.6 0.0 copy-start
  0.6 0.7 reshape.32
  1.4 0.8 copy.15
  2.1 0.6 reshape.28.table
  2.7 0.8 copy.14
  3.6 0.7 reshape.27.shocks
  4.3 0.0 copy-start.3
  4.3 0.8 copy-done.3
  5.0 7.3 %shard_map.119 = (bf16[2,384,256]{2,1,0:T(8,128)(2,1)S(1)}, bf16[2,384,256]{2,1,0:T(8,128)(2,1)S(1)}, f32[32,256]{1,0:T(8,128)S(1)}, f32[32,256]{1,0:T(8,128)S(1)}) custom-call(f32[6144,256]{1,0:T(8,128)} %bitcast.20, f32[6144,256]{1,0:T(8,128)} %bitcast.21, f32[32,256]{1,0:T(8,128)S(1)} %bitcast.19), custom_call_target="tpu_custom_call" | custom-call | tf_op jit(solution)/shard_map/pallas_call | solution.py:115
  12.3 0.0 copy-start.1
  12.4 0.7 copy-done.1
  13.1 0.0 copy-start.2
  13.1 0.7 copy-done.2
  13.8 0.0 copy-start.4
  13.8 0.6 copy-done.4
  14.4 0.0 copy-start.5
  14.4 0.6 copy-done.5
  15.0 24.1 %shard_map.120 = (f32[6144,256]{1,0:T(8,128)}, bf16[384,4096]{1,0:T(8,128)(2,1)}) custom-call(s32[768]{0:T(1024)} %reshape.27.shocks, f32[16]{0:T(128)} %reshape.28.table, f32[6144,256]{1,0:T(8,128)} %bitcast.22, bf16[2,384,256]{2,1,0:T(8,128)(2,1)} %copy-done.1, bf16[2,384,256]{2,1,0:T(8,128)(2,1)} %copy-done.2, f32[32,256]{1,0:T(8,128)} %bitcast.18, ...), custom_call_target="tpu_custom_call" | custom-call | tf_op jit(solution)/shard_map/pallas_call | solution.py:229
  39.2 11.1 %fusion.5.refs_0_ = f32[384,2048]{1,0:T(8,128)S(1)} fusion(bf16[384,4096]{1,0:T(8,128)(2,1)} %get-tuple-element.18, bf16[4096,2048]{1,0:T(8,128)(2,1)} %param.12), kind=kOutput, calls=%fused_computation.12 | convolution fusion | flops 6442450944 | bytes 23068672 | tf_op jit(solution)/shard_map/dot_general | solution.py:423
  50.3 0.0 copy-start.7
  50.3 0.0 copy-start.6
  50.3 47.3 %shard_map.121.refs_1_ = bf16[384,2048]{1,0:T(8,128)(2,1)S(1)} custom-call(f32[384,2048]{1,0:T(8,128)S(1)} %fusion.5.refs_0_), custom_call_target="tpu_custom_call" | custom-call | tf_op jit(solution)/shard_map/pallas_call | solution.py:400
  97.7 0.0 copy-done
  97.7 0.6 fusion
  98.3 0.7 convolution_bitcast_fusion.1
  98.9 0.0 copy-done.7
  98.9 0.2 convolution_bitcast_fusion.refs_2_
  99.1 0.0 copy-done.6
  99.1 1.5 convolution_convert_fusion.1
  100.7 2.3 %fusion.1.refs_0_ = f32[384,2048]{1,0:T(8,128)} fusion(bf16[2048,128]{1,0:T(8,128)(2,1)S(1)} %copy-done, bf16[384,128]{1,0:T(8,128)(2,1)S(1)} %fusion, f32[128]{0:T(128)S(1)} %copy-done.7, f32[384]{0:T(512)S(1)} %copy-done.6), kind=kOutput, calls=%fused_computation.7 | convolution fusion | flops 201621504 | bytes 3770368 | tf_op jit(solution)/shard_map/dot_general | solution.py:436
  102.9 0.0 copy-start.8
  102.9 41.0 %shard_map.122 = (bf16[384,2048]{1,0:T(8,128)(2,1)S(1)}, f32[8,384]{1,0:T(8,128)S(1)}) custom-call(f32[384,2048]{1,0:T(8,128)} %fusion.1.refs_0_, bf16[384,2048]{1,0:T(8,128)(2,1)S(1)} %shard_map.121.refs_1_, f32[8,384]{1,0:T(8,128)S(1)} %convolution_bitcast_fusion.refs_2_), custom_call_target="tpu_custom_call" | custom-call | tf_op jit(solution)/shard_map/pallas_call | solution.py:400
  143.9 0.6 slice_reduce_fusion
  144.5 0.0 copy-done.8
  144.5 12.6 %convolution_convert_fusion = bf16[4096,2048]{1,0:T(8,128)(2,1)} fusion(bf16[384,4096]{1,0:T(8,128)(2,1)S(1)} %copy-done.8, bf16[384,2048]{1,0:T(8,128)(2,1)S(1)} %get-tuple-element.20), kind=kOutput, calls=%fused_computation | convolution fusion | flops 6450839552 | bytes 21495808 | tf_op jit(solution)/shard_map/dot_general | solution.py:443
Async XLA Ops:
  0.6 97.0 %copy-start = (bf16[2048,128]{1,0:T(8,128)(2,1)S(1)}, bf16[2048,128]{1,0:T(8,128)(2,1)}, u32[]{:S(2)}) copy-start(bf16[2048,128]{1,0:T(8,128)(2,1)} %param.13) | copy-start | bytes 1572868
  4.3 0.8 copy-start.3
  12.3 0.7 copy-start.1
  13.1 0.7 copy-start.2
  13.8 0.6 copy-start.4
  14.4 0.6 copy-start.5
  50.3 48.7 %copy-start.7 = (f32[128]{0:T(128)S(1)}, f32[128]{0:T(128)}, u32[]{:S(2)}) copy-start(f32[128]{0:T(128)} %param.14) | copy-start | bytes 1540
  50.3 48.8 %copy-start.6 = (f32[384]{0:T(512)S(1)}, f32[384]{0:T(512)}, u32[]{:S(2)}) copy-start(f32[384]{0:T(512)} %param.15) | copy-start | bytes 4612
  102.9 41.6 %copy-start.8 = (bf16[384,4096]{1,0:T(8,128)(2,1)S(1)}, bf16[384,4096]{1,0:T(8,128)(2,1)}, u32[]{:S(2)}) copy-start(bf16[384,4096]{1,0:T(8,128)(2,1)} %get-tuple-element.18) | copy-start | bytes 9437188

commit v2 on v1

--- a/solution.py
+++ b/solution.py
@@ -131,10 +131,9 @@
 
 
 def stencil_kernel(
-    n, rows, extended, steps, shocks, table, x_ref, lo_ref, hi_ref, drift_ref, dlo_ref, dhi_ref,
+    n, rows, extended, steps, block, shocks, table, x_ref, lo_ref, hi_ref, drift_ref, dlo_ref, dhi_ref,
     out_ref, flat_ref, coef, *strips
 ):
-    block = lo_ref.shape[1]
     columns = x_ref.shape[1]
     stored = x_ref.shape[0] // block
     extra = extended - stored
@@ -164,12 +163,13 @@
         for strip in halo_rows:
             strip[...] = jnp.zeros_like(strip)
 
+    now = pl.ds(pl.multiple_of(first_no, 8), block)
     for k in range(lanes if extra else 0):
         part = slice(k * 128, (k + 1) * 128)
         for i in range(2):
-            halo_rows[k][pl.ds(i, block, stride=extra), :] = hi_ref[i, :, part].astype(F32)
+            halo_rows[k][pl.ds(i, block, stride=extra), :] = hi_ref[i, now, part].astype(F32)
             halo_rows[k][pl.ds(extra - 2 + i, block, stride=extra), :] = lo_ref[
-                i, :, part
+                i, now, part
             ].astype(F32)
 
     row = lax.broadcasted_iota(jnp.int32, (extended, columns), 0)
@@ -184,8 +184,8 @@
             ends = jnp.concatenate([strip[at, :] for strip in halo_rows], axis=1)
             c = jnp.concatenate([c, ends], axis=0)
         for t in range(steps):
-            level = shocks[(first_no + s) * steps + t]
-            half_x, half_y = 0.5 * table[2 * level], 0.5 * table[2 * level + 1]
+            level = shocks[t, first_no + s]
+            half_x, half_y = 0.5 * table[0, level], 0.5 * table[1, level]
             above = (coef[0] - half_x) * c
             below = (coef[1] + half_x) * c
             left = (coef[2] - half_y * not_first) * c
@@ -223,17 +223,15 @@
         x3 = x2.reshape(count, rows, columns)
         x2 = jnp.concatenate([x3, after, filler, before], axis=1).reshape(-1, columns)
     block = max(b for b in (8, 16, 32) if count % b == 0)
-    whole = pl.BlockSpec(drift2.shape, lambda i: (0, 0))
-    edge = pl.BlockSpec((2, block, columns), lambda i: (0, i, 0))
     cells = pl.BlockSpec((block * stored, columns), lambda i: (i, 0))
     density, flat = pl.pallas_call(
-        functools.partial(stencil_kernel, n, rows, extended, steps),
+        functools.partial(stencil_kernel, n, rows, extended, steps, block),
         grid=(count // block,),
         out_shape=(
             jax.ShapeDtypeStruct(x2.shape, F32),
             jax.ShapeDtypeStruct((count, rows * columns), BF16),
         ),
-        in_specs=[SMEM, SMEM, cells, edge, edge, whole, whole, whole],
+        in_specs=[SMEM, SMEM, cells] + [VMEM] * 5,
         out_specs=(cells, pl.BlockSpec((block, rows * columns), lambda i: (i, 0))),
         scratch_shapes=[
             pltpu.VMEM((4, extended, columns), F32),
@@ -268,7 +266,7 @@
     streams = len(orders)
     got = [[refs.pop(0) for _ in range(stages)] for _ in range(streams)]
     acc = [[refs.pop(0) for _ in range(stages - 1)] + [None] for _ in range(streams)]
-    narrow = [[None] * wide + [refs.pop(0) for _ in range(wide, stages)] for _ in range(streams)]
+    narrow = [[None if s in wide else refs.pop(0) for s in range(stages)] for _ in range(streams)]
     if second_pass:
         v_got, v_acc = refs.pop(0), refs.pop(0)
         v_send, v_recv = refs.pop(0), refs.pop(0)
@@ -294,7 +292,7 @@
             if dim == 1:
                 col = pl.multiple_of(col + bit * c, 128)
             else:
-                row = pl.multiple_of(row + bit * r, 16)
+                row = pl.multiple_of(row + bit * r, 8)
             spots.append((pl.ds(row, r), pl.ds(col, c)))
         place.append(spots)
 
@@ -304,18 +302,18 @@
         if dim == 1:
             at_col = pl.multiple_of(which * c, 128)
         else:
-            at_row = pl.multiple_of(at_row + which * r, 16)
+            at_row = pl.multiple_of(at_row + which * r, 8)
         return (x_ref if s == 0 else acc[t][s - 1]), (pl.ds(at_row, r), pl.ds(at_col, c))
 
     def scatter(t, s):
         b = orders[t][s]
         ref, spot = half(t, s, 1 - bits[b])
         sem = t * 2 * stages + s
-        src = ref.at[spot] if s < wide else narrow[t][s]
+        src = ref.at[spot] if s in wide else narrow[t][s]
         return remote(src, got[t][s], send.at[sem], recv.at[sem], partner[b])
 
     def begin(t, s):
-        if s >= wide:
+        if s not in wide:
             ref, spot = half(t, s, 1 - bits[orders[t][s]])
             narrow[t][s][...] = ref[spot].astype(BF16)
         scatter(t, s).start()
@@ -374,25 +372,30 @@
 def reduce_gather(n, x, wide, first=None, v=None):
     stages = n.bit_length() - 1
     assert n == 1 << stages
-    streams = 2
+    streams = 4
     plan = halvings(x.shape[0] // streams, x.shape[1], stages)
-    orders = [list(range(stages)), list(range(stages))]
+    orders = [list(range(stages)) for _ in range(streams)]
     if stages > 2:
-        orders[1][1:3] = [2, 1]
+        for order in orders[1::2]:
+            order[1:3] = [2, 1]
     second_pass = first is not None
     out_shape = [jax.ShapeDtypeStruct(x.shape, BF16)]
     operands = [x]
     if second_pass:
         out_shape.append(jax.ShapeDtypeStruct(v.shape, F32))
         operands += [first, v]
-    wide = min(wide, stages)
     scratch = [
-        pltpu.VMEM(p[1:], F32 if s < wide else BF16)
+        pltpu.VMEM(p[1:], F32 if s in wide else BF16)
         for _ in range(streams)
         for s, p in enumerate(plan)
     ]
     scratch += [pltpu.VMEM(p[1:], F32) for _ in range(streams) for p in plan[:-1]]
-    scratch += [pltpu.VMEM(p[1:], BF16) for _ in range(streams) for p in plan[wide:]]
+    scratch += [
+        pltpu.VMEM(p[1:], BF16)
+        for _ in range(streams)
+        for s, p in enumerate(plan)
+        if s not in wide
+    ]
     if second_pass:
         scratch += [pltpu.VMEM((stages,) + v.shape, F32)] * 2
         scratch += [pltpu.SemaphoreType.DMA((stages,))] * 2
@@ -417,11 +420,11 @@
     drift2 = drift.reshape(2 * row_count, columns)
     lo, hi, dlo, dhi = halo(n, row_count, x2, drift2)
     density, inputs = stencil(
-        n, row_count, shocks.shape[1], shocks.reshape(-1), shock_table.reshape(-1),
+        n, row_count, shocks.shape[1], shocks.T, shock_table.T,
         x2, lo, hi, drift2, dlo, dhi,
     )
     partial_first = jnp.dot(inputs, first_weight, preferred_element_type=F32)
-    (first_act,) = reduce_gather(n, partial_first, 2)
+    (first_act,) = reduce_gather(n, partial_first, (0, 2))
     second_pre = jnp.dot(first_act, mid_weight, preferred_element_type=F32)
     second_act = jnp.tanh(second_pre).astype(BF16)
     second_f = second_act.astype(F32)
@@ -436,7 +439,7 @@
     back_part = lax.dot_general(
         back_second, mid_weight, (((1,), (1,)), ((), ())), preferred_element_type=F32
     )
-    back_first, value = reduce_gather(n, back_part, 1, first_act, value_part)
+    back_first, value = reduce_gather(n, back_part, (0,), first_act, value_part)
     grad_mid = lax.dot_general(
         first_act, back_second, (((0,), (0,)), ((), ())), preferred_element_type=F32
     )

time: 157 us -> 143 us (0.911)
  Pallas kernels: 120 us -> 108 us
  local copies, waits for them, and re-layouts: 7.69 us -> 4.8 us
    pallas_call x2, Pallas kernels: 88.3 us -> 75.7 us  [reduce_gather(): pl.pallas_call(functools.partial(reduce_kernel, n, plan, orders, wide, se...]
    unnamed x21 -> x19, local copies, waits for them, and re-layouts: 5.77 us -> 4.2 us
where the time goes in v2:
time: 143 us; the launch traced here: 142 us
  Pallas kernels  108 us (76%)
  matrix products  28.9 us (20%)
  local copies, waits for them, and re-layouts  4.8 us (3%)
    pallas_call x2, Pallas kernels, reduce_gather(): pl.pallas_call(functools.partial(reduce_kernel, n, plan, orders, wide, se...  75.7 us
    pallas_call x1, Pallas kernels, stencil(): pl.pallas_call(functools.partial(stencil_kernel, n, rows, extended, steps...  24.9 us
    dot_general x1, matrix products, local(): lax.dot_general(inputs, back_first, (((0,), (0,)), ((), ())), preferred_e...  12.6 us
    dot_general x1, matrix products, local(): partial_first = jnp.dot(inputs, first_weight, preferred_element_type=F32)  11.1 us
    pallas_call x1, Pallas kernels, halo(): pl.pallas_call(functools.partial(halo_kernel, n, rows, lanes), grid=(1,),...  7.29 us
    unnamed x19, local copies, waits for them, and re-layouts  4.2 us

profile of v2, /device:TPU:0, one launch (start us, length us, event | category | flops | bytes accessed | tf_op | source)
XLA Modules:
  0.0 142.4 jit_solution(5721011448692668990)
XLA Ops:
  0.6 0.0 copy-start
  0.6 0.7 reshape.24
  1.4 0.0 copy-start.3
  1.4 0.8 copy-done.3
  2.1 7.3 %shard_map.119 = (bf16[2,384,256]{2,1,0:T(8,128)(2,1)S(1)}, bf16[2,384,256]{2,1,0:T(8,128)(2,1)S(1)}, f32[32,256]{1,0:T(8,128)S(1)}, f32[32,256]{1,0:T(8,128)S(1)}) custom-call(f32[6144,256]{1,0:T(8,128)} %bitcast.22, f32[6144,256]{1,0:T(8,128)} %bitcast.23, f32[32,256]{1,0:T(8,128)S(1)} %bitcast.21), custom_call_target="tpu_custom_call" | custom-call | tf_op jit(solution)/shard_map/pallas_call | solution.py:115
  9.4 0.0 copy-start.1
  9.5 0.7 copy-done.1
  10.2 0.0 copy-start.2
  10.2 0.7 copy-done.2
  10.9 0.0 copy-start.4
  10.9 0.6 copy-done.4
  11.5 0.0 copy-start.5
  11.5 0.6 copy-done.5
  12.1 24.9 %shard_map.120 = (f32[6144,256]{1,0:T(8,128)}, bf16[384,4096]{1,0:T(8,128)(2,1)}) custom-call(s32[2,384]{1,0:T(2,128)} %bitcast.25, f32[2,8]{1,0:T(2,128)} %bitcast.26, f32[6144,256]{1,0:T(8,128)} %bitcast.24, bf16[2,384,256]{2,1,0:T(8,128)(2,1)} %copy-done.1, bf16[2,384,256]{2,1,0:T(8,128)(2,1)} %copy-done.2, f32[32,256]{1,0:T(8,128)} %bitcast.20, ...), custom_call_target="tpu_custom_call" | custom-call | tf_op jit(solution)/shard_map/pallas_call | solution.py:227
  37.0 11.1 %fusion.5.refs_0_ = f32[384,2048]{1,0:T(8,128)S(1)} fusion(bf16[384,4096]{1,0:T(8,128)(2,1)} %get-tuple-element.18, bf16[4096,2048]{1,0:T(8,128)(2,1)} %param.12), kind=kOutput, calls=%fused_computation.12 | convolution fusion | flops 6442450944 | bytes 23068672 | tf_op jit(solution)/shard_map/dot_general | solution.py:426
  48.2 0.0 copy-start.7
  48.2 0.0 copy-start.6
  48.2 42.5 %shard_map.121.refs_1_ = bf16[384,2048]{1,0:T(8,128)(2,1)S(1)} custom-call(f32[384,2048]{1,0:T(8,128)S(1)} %fusion.5.refs_0_), custom_call_target="tpu_custom_call" | custom-call | tf_op jit(solution)/shard_map/pallas_call | solution.py:403
  90.7 0.0 copy-done
  90.8 0.6 fusion
  91.3 0.7 convolution_bitcast_fusion.1
  92.0 0.0 copy-done.7
  92.0 0.2 convolution_bitcast_fusion.refs_2_
  92.2 0.0 copy-done.6
  92.2 1.5 %convolution_convert_fusion.1 = bf16[2048,128]{1,0:T(8,128)(2,1)} fusion(bf16[384,2048]{1,0:T(8,128)(2,1)S(1)} %shard_map.121.refs_1_, bf16[384,128]{1,0:T(8,128)(2,1)S(1)} %fusion, f32[128]{0:T(128)S(1)} %copy-done.7, f32[384]{0:T(512)S(1)} %copy-done.6), kind=kOutput, calls=%fused_computation.1 | convolution fusion | flops 201883648 | bytes 2197504 | tf_op jit(solution)/shard_map/dot_general | solution.py:443
  93.7 2.3 %fusion.1.refs_0_ = f32[384,2048]{1,0:T(8,128)} fusion(bf16[2048,128]{1,0:T(8,128)(2,1)S(1)} %copy-done, bf16[384,128]{1,0:T(8,128)(2,1)S(1)} %fusion, f32[128]{0:T(128)S(1)} %copy-done.7, f32[384]{0:T(512)S(1)} %copy-done.6), kind=kOutput, calls=%fused_computation.7 | convolution fusion | flops 201621504 | bytes 3770368 | tf_op jit(solution)/shard_map/dot_general | solution.py:439
  96.0 0.0 copy-start.8
  96.0 33.2 %shard_map.122 = (bf16[384,2048]{1,0:T(8,128)(2,1)S(1)}, f32[8,384]{1,0:T(8,128)S(1)}) custom-call(f32[384,2048]{1,0:T(8,128)} %fusion.1.refs_0_, bf16[384,2048]{1,0:T(8,128)(2,1)S(1)} %shard_map.121.refs_1_, f32[8,384]{1,0:T(8,128)S(1)} %convolution_bitcast_fusion.refs_2_), custom_call_target="tpu_custom_call" | custom-call | tf_op jit(solution)/shard_map/pallas_call | solution.py:403
  129.2 0.6 slice_reduce_fusion
  129.8 0.0 copy-done.8
  129.8 12.6 %convolution_convert_fusion = bf16[4096,2048]{1,0:T(8,128)(2,1)} fusion(bf16[384,4096]{1,0:T(8,128)(2,1)S(1)} %copy-done.8, bf16[384,2048]{1,0:T(8,128)(2,1)S(1)} %get-tuple-element.20), kind=kOutput, calls=%fused_computation | convolution fusion | flops 6450839552 | bytes 21495808 | tf_op jit(solution)/shard_map/dot_general | solution.py:446
Async XLA Ops:
  0.6 90.1 %copy-start = (bf16[2048,128]{1,0:T(8,128)(2,1)S(1)}, bf16[2048,128]{1,0:T(8,128)(2,1)}, u32[]{:S(2)}) copy-start(bf16[2048,128]{1,0:T(8,128)(2,1)} %param.13) | copy-start | bytes 1572868
  1.4 0.8 copy-start.3
  9.4 0.7 copy-start.1
  10.2 0.7 copy-start.2
  10.9 0.6 copy-start.4
  11.5 0.6 copy-start.5
  48.2 43.9 %copy-start.7 = (f32[128]{0:T(128)S(1)}, f32[128]{0:T(128)}, u32[]{:S(2)}) copy-start(f32[128]{0:T(128)} %param.14) | copy-start | bytes 1540
  48.2 44.0 %copy-start.6 = (f32[384]{0:T(512)S(1)}, f32[384]{0:T(512)}, u32[]{:S(2)}) copy-start(f32[384]{0:T(512)} %param.15) | copy-start | bytes 4612
  96.0 33.8 %copy-start.8 = (bf16[384,4096]{1,0:T(8,128)(2,1)S(1)}, bf16[384,4096]{1,0:T(8,128)(2,1)}, u32[]{:S(2)}) copy-start(bf16[384,4096]{1,0:T(8,128)(2,1)} %get-tuple-element.18) | copy-start | bytes 9437188
